TPU v7x, 128 devices: a whole 4x4x4 slice. The times are simulated.
128 devices in a mesh: patch: 8 (over x, core), proto: 16 (over z, y).
Axes of the slice: x: 4, y: 4, z: 4, core: 2. Of those that a mesh axis runs over, the one named last changes fastest.
Arguments:
- student_feats: bfloat16 [32768, 256], P(('patch', 'proto')), may hold values from -50 to 50
- teacher_feats: bfloat16 [32768, 256], P(('patch', 'proto')), may hold values from -50 to 50
- proto_weight: bfloat16 [256, 131072], P(None, 'proto'), may hold values from -4 to 4
- mask_index: int32 [4096], P(('patch', 'proto')), may hold values from 0 to 255, as said below
- row_weight: bfloat16 [4096], P(('patch', 'proto')), may hold values from 0.5 to 4
Outputs:
- grad_student: float32 [4096, 256], P(('patch', 'proto'))
- grad_proto: float32 [256, 131072], P('patch', 'proto')
- loss: float32 [], replicated
Inputs may be any that keep to these rules, and one draw needn't show every extreme that they name: `mask_index`: entries k * 32 to (k + 1) * 32 - 1 are distinct patch positions of image k, counted from that image's first patch.
All inputs are finite; a program needn't handle non-finite values.
Results may differ from a plain program's by a relative error of at most 0.0057.
Values may be sent and summed in bfloat16 or wider, within the bound.
No kernel may reach another device: no remote copies, remote signals or barrier semaphores. Data moves between devices by JAX's collectives and lax.ppermute only.
A program may use at most 128 MiB of HBM per device.

v0:
```python
import jax
import jax.numpy as jnp
from jax import lax
from jax.sharding import PartitionSpec as P

SK_ITERS = 3
eps = 1e-06
teacher_temp = 0.07
student_temp = 0.1


def unit_rows(values):
    values = values.astype(jnp.float32)
    inverse = lax.rsqrt(jnp.sum(values * values, axis=1) + eps)
    return (values * inverse[:, None], inverse)


def finish(teacher_exp, scale_rows, scale_cols, logits, exp_logits, exp_total, weights):
    codes = teacher_exp * scale_rows[:, None] * scale_cols[None, :]
    student_probs = exp_logits / exp_total[:, None]
    grad_logits = (weights[:, None] * (student_probs - codes)).astype(jnp.bfloat16)
    log_total = jnp.log(exp_total)
    loss_partial = jnp.sum(weights[:, None] * codes * (log_total[:, None] - logits))
    return (grad_logits, loss_partial)


def feature_term(grad_logits, proto_cols):
    return (
        lax.dot_general(
            grad_logits, proto_cols, (((1,), (1,)), ((), ())), preferred_element_type=jnp.float32
        )
        / student_temp
    )


def head_term(student_rows, grad_logits):
    return (
        lax.dot_general(
            student_rows, grad_logits, (((0,), (0,)), ((), ())), preferred_element_type=jnp.float32
        )
        / student_temp
    )


def on_device(student_feats, teacher_feats, proto_weight, mask_index, row_weight):
    highest = lax.Precision.HIGHEST
    unit_student, inverse_student = unit_rows(jnp.take(student_feats, mask_index, axis=0))
    unit_teacher, _ = unit_rows(jnp.take(teacher_feats, mask_index, axis=0))
    own_student = unit_student.astype(jnp.bfloat16)
    own_teacher = unit_teacher.astype(jnp.bfloat16)
    w_float = proto_weight.astype(jnp.float32)
    col_inverse = lax.rsqrt(jnp.sum(w_float * w_float, axis=0) + eps)
    unit_proto = w_float * col_inverse[None, :]
    proto_unit = unit_proto.astype(jnp.bfloat16)
    teacher_rows, student_rows, weights = (
        lax.all_gather(own_teacher, "proto", axis=0, tiled=True),
        lax.all_gather(own_student, "proto", axis=0, tiled=True),
        lax.all_gather(row_weight, "proto", axis=0, tiled=True),
    )
    weights = weights.astype(jnp.float32)
    teacher_exp = jnp.exp(
        jnp.dot(teacher_rows, proto_unit, preferred_element_type=jnp.float32) / teacher_temp
    )
    scale_rows = jnp.ones((teacher_rows.shape[0],), jnp.float32)
    for sweep in range(SK_ITERS):
        col_part = jnp.dot(scale_rows, teacher_exp, precision=highest)
        scale_cols = 1.0 / lax.psum(col_part, "patch")
        row_part = jnp.dot(teacher_exp, scale_cols, precision=highest)
        scale_rows = 1.0 / lax.psum(row_part, "proto")
    logits = jnp.dot(student_rows, proto_unit, preferred_element_type=jnp.float32) / student_temp
    exp_logits = jnp.exp(logits)
    exp_total = lax.psum(jnp.sum(exp_logits, axis=1), "proto")
    grad_logits, loss_partial = finish(
        teacher_exp, scale_rows, scale_cols, logits, exp_logits, exp_total, weights
    )
    feature_grad = lax.psum_scatter(
        feature_term(grad_logits, proto_unit), "proto", scatter_dimension=0, tiled=True
    )
    row_share = proto_unit.shape[0] // lax.axis_size("patch")
    row_offset = lax.axis_index("patch") * row_share
    head_full = lax.psum(head_term(student_rows, grad_logits), "patch")
    inner = jnp.sum(unit_proto * head_full, axis=0)
    whole_grad = col_inverse[None, :] * (head_full - unit_proto * inner[None, :])
    grad_proto = lax.dynamic_slice_in_dim(whole_grad, row_offset, row_share, 0)
    loss_total, weight_total = lax.psum(
        (loss_partial, jnp.sum(row_weight.astype(jnp.float32))), ("patch", "proto")
    )
    grad_student = inverse_student[:, None] * (
        feature_grad - unit_student * jnp.sum(unit_student * feature_grad, axis=1)[:, None]
    )
    return (grad_student, grad_proto, loss_total / weight_total)


def solution(mesh):
    in_specs = (
        P(("patch", "proto"), None),
        P(("patch", "proto"), None),
        P(None, "proto"),
        P(("patch", "proto")),
        P(("patch", "proto")),
    )
    out_specs = (P(("patch", "proto"), None), P("patch", "proto"), P())
    return jax.shard_map(
        on_device, mesh=mesh, in_specs=in_specs, out_specs=out_specs, check_vma=False
    )
```

profile of v0, /device:TPU:1, one launch (start us, length us, event | category | flops | bytes accessed | tf_op | source)
XLA Modules:
  0.0 526.8 jit_solution(3142531026962949100)
XLA Ops:
  8.1 0.7 compare_select_fusion
  8.7 0.7 compare_and_fusion
  9.4 0.6 gather_fusion
  10.1 1.5 gather_fusion.1
  11.9 20.8 %all_gather.11 = bf16[512,256]{1,0:T(8,128)(2,1)S(1)} all-gather(bf16[32,256]{1,0:T(8,128)(2,1)S(1)} %get-tuple-element.15), channel_id=1, replica_groups=mesh['patch'=8,'proto'=16] {'proto'}, dimensions={0}, use_global_device_ids=true | all-gather | bytes 278528 | tf_op jit(solution)/shard_map/all_gather | solution.py:56
  32.7 3.1 fusion
  35.8 4.5 multiply_exponential_fusion
  40.3 7.9 %fusion.20 = f32[1,8192]{1,0:T(1,128)S(1)} fusion(f32[512,8192]{1,0:T(8,128)S(1)} %multiply_exponential_fusion), kind=kOutput, calls=%fused_computation.41 | convolution fusion | flops 50331648 | bytes 16809984 | tf_op jit(solution)/shard_map/dot_general | solution.py:66
  48.2 26.1 %psum.71 = f32[8192]{0:T(1024)S(1)} all-reduce(f32[8192]{0:T(1024)S(1)} %bitcast.33), channel_id=1, replica_groups=mesh['patch'=8,'proto'=16] {'patch'}, use_global_device_ids=true, to_apply=%region_5.7 | all-reduce | flops 8192 | bytes 65536 | tf_op jit(solution)/shard_map/psum | solution.py:67
  74.4 17.6 %fusion.23 = f32[1,512]{1,0:T(1,128)S(1)} fusion(f32[512,8192]{1,0:T(8,128)} %copy-done.2, f32[8192,1]{0,1:T(1,128)S(1)} %bitcast.29), kind=kOutput, calls=%fused_computation.50 | convolution fusion | flops 50331648 | bytes 16812032 | tf_op jit(solution)/shard_map/dot_general | solution.py:68
  92.0 31.0 %psum.72 = f32[512]{0:T(512)S(1)} all-reduce(f32[512]{0:T(512)S(1)} %bitcast.35), channel_id=1, replica_groups=mesh['patch'=8,'proto'=16] {'proto'}, use_global_device_ids=true, to_apply=%region_6.8 | all-reduce | flops 512 | bytes 4096 | tf_op jit(solution)/shard_map/psum | solution.py:69
  123.0 11.5 %fusion.24 = f32[1,8192]{1,0:T(1,128)S(1)} fusion(f32[512,1]{0,1:T(1,128)S(1)} %bitcast.37, f32[512,8192]{1,0:T(8,128)} %copy-done.2), kind=kOutput, calls=%fused_computation.51 | convolution fusion | flops 50331648 | bytes 16812032 | tf_op jit(solution)/shard_map/dot_general | solution.py:66
  134.5 30.9 %psum.73 = f32[8192]{0:T(1024)S(1)} all-reduce(f32[8192]{0:T(1024)S(1)} %bitcast.30), channel_id=1, replica_groups=mesh['patch'=8,'proto'=16] {'patch'}, use_global_device_ids=true, to_apply=%region_7.9 | all-reduce | flops 8192 | bytes 65536 | tf_op jit(solution)/shard_map/psum | solution.py:67
  165.4 17.6 %fusion.25 = f32[1,512]{1,0:T(1,128)S(1)} fusion(f32[512,8192]{1,0:T(8,128)} %copy-done.2, f32[8192,1]{0,1:T(1,128)S(1)} %bitcast.31), kind=kOutput, calls=%fused_computation.52 | convolution fusion | flops 50331648 | bytes 16812032 | tf_op jit(solution)/shard_map/dot_general | solution.py:68
  183.0 28.5 %psum.74 = f32[512]{0:T(512)S(1)} all-reduce(f32[512]{0:T(512)S(1)} %bitcast.36), channel_id=1, replica_groups=mesh['patch'=8,'proto'=16] {'proto'}, use_global_device_ids=true, to_apply=%region_8.10 | all-reduce | flops 512 | bytes 4096 | tf_op jit(solution)/shard_map/psum | solution.py:69
  211.5 11.5 %fusion.26 = f32[1,8192]{1,0:T(1,128)S(1)} fusion(f32[512,1]{0,1:T(1,128)S(1)} %bitcast.38, f32[512,8192]{1,0:T(8,128)} %copy-done.2), kind=kOutput, calls=%fused_computation.53 | convolution fusion | flops 50331648 | bytes 16812032 | tf_op jit(solution)/shard_map/dot_general | solution.py:66
  223.0 31.0 %psum.75 = f32[8192]{0:T(1024)S(1)} all-reduce(f32[8192]{0:T(1024)S(1)} %bitcast.32), channel_id=1, replica_groups=mesh['patch'=8,'proto'=16] {'patch'}, use_global_device_ids=true, to_apply=%region_9.11 | all-reduce | flops 8192 | bytes 65536 | tf_op jit(solution)/shard_map/psum | solution.py:67
  254.0 17.8 %fusion.27 = f32[1,512]{1,0:T(1,128)S(1)} fusion(f32[512,8192]{1,0:T(8,128)} %copy-done.2, f32[8192,1]{0,1:T(1,128)S(1)} %bitcast.28), kind=kOutput, calls=%fused_computation.54 | convolution fusion | flops 50331648 | bytes 16812032 | tf_op jit(solution)/shard_map/dot_general | solution.py:68
  271.7 17.8 %all_gather.10 = bf16[512,256]{1,0:T(8,128)(2,1)S(1)} all-gather(bf16[32,256]{1,0:T(8,128)(2,1)S(1)} %get-tuple-element.14), channel_id=1, replica_groups=mesh['patch'=8,'proto'=16] {'proto'}, dimensions={0}, use_global_device_ids=true | all-gather | bytes 278528 | tf_op jit(solution)/shard_map/all_gather | solution.py:57
  289.5 7.5 %exponential_reduce_fusion = (f32[512]{0:T(512)S(1)}, f32[512,8192]{1,0:T(8,128)}) fusion(bf16[512,256]{1,0:T(8,128)(2,1)S(1)} %all_gather.10, f32[8192]{0:T(1024)S(1)} %add_rsqrt_fusion, bf16[256,8192]{1,0:T(8,128)(2,1)S(1)} %copy-done.3), kind=kOutput, calls=%fused_computation.6 | convolution fusion | flops 2162163200 | bytes 21268480 | tf_op jit(solution)/shard_map/dot_general | solution.py:70
  297.0 30.9 %all-reduce.2 = (f32[512]{0:T(512)S(1)}, f32[512]{0:T(512)S(1)}) all-reduce(f32[512]{0:T(512)S(1)} %bitcast.34, f32[512]{0:T(512)S(1)} %get-tuple-element.16), channel_id=1, replica_groups=mesh['patch'=8,'proto'=16] {'proto'}, use_global_device_ids=true, to_apply=%region_10.12 | all-reduce | flops 1024 | bytes 8192 | tf_op jit(solution)/shard_map/psum | solution.py:69
  329.4 29.0 %all-reduce = bf16[512]{0:T(512)(128)(2,1)S(1)} all-reduce(bf16[512]{0:T(512)(128)(2,1)S(1)} %dynamic-update-slice), channel_id=1, replica_groups=mesh['patch'=8,'proto'=16] {'proto'}, use_global_device_ids=true, to_apply=%add | all-reduce | flops 512 | bytes 2048
  358.4 14.4 %multiply_reduce_fusion = (f32[]{:T(128)}, bf16[512,8192]{1,0:T(8,128)(2,1)S(1)}) fusion(f32[512,8192]{1,0:T(8,128)} %copy-done.2, f32[512,8192]{1,0:T(8,128)} %get-tuple-element.17, f32[512]{0:T(512)S(1)} %log.3, f32[8192]{0:T(1024)S(1)} %broadcast_divide_fusion, f32[512]{0:T(512)S(1)} %broadcast_divide_fusion.5, f32[512]{0:T(512)S(1)} %convert_element_type.28, ...), kind=kLoop, calls=%fused_computation.2 | loop fusion | flops 46137344 | bytes 41984004 | tf_op jit(solution)/shard_map/reduce_sum | solution.py:23
  372.9 3.2 copy-done.5
  376.1 3.2 fusion.7
  379.4 9.0 %convolution_multiply_fusion = f32[256,8192]{1,0:T(8,128)} fusion(bf16[512,256]{1,0:T(8,128)(2,1)S(1)} %all_gather.10, bf16[512,8192]{1,0:T(8,128)(2,1)} %copy-done.5), kind=kOutput, calls=%fused_computation.7 | convolution fusion | flops 2149580800 | bytes 17039360 | tf_op jit(solution)/shard_map/dot_general | solution.py:38
  389.0 85.0 %all-reduce.1 = (f32[]{:T(128)}, f32[]{:T(128)}) all-reduce(f32[]{:T(128)} %get-tuple-element.10, f32[]{:T(128)} %convert_reduce_fusion), channel_id=1, replica_groups=mesh['patch'=8,'proto'=16] {'patch','proto'}, use_global_device_ids=true, to_apply=%region_16.18 | all-reduce | flops 2 | bytes 16 | tf_op jit(solution)/shard_map/psum | solution.py:85
  475.3 0.9 fusion.14
  476.3 1.5 fusion.16
  477.8 32.0 %all-reduce.5.cloned.1.call-done = f32[256,8192]{1,0:T(8,128)} async-done(((f32[256,8192]{1,0:T(8,128)}), f32[256,8192]{1,0:T(8,128)}) %all-reduce.5.cloned.1.call-update) | async-done | bytes 8388624 | tf_op jit(solution)/shard_map/psum | solution.py:81
  509.8 6.0 %multiply_reduce_fusion.1 = (f32[8192]{0:T(1024)S(1)}, f32[256,8192]{1,0:T(8,128)S(1)}) fusion(f32[256,8192]{1,0:T(8,128)} %all-reduce.5.cloned.1.call-done, f32[8192]{0:T(1024)S(1)} %add_rsqrt_fusion, bf16[256,8192]{1,0:T(8,128)(2,1)} %param.9), kind=kLoop, calls=%fused_computation.11 | loop fusion | flops 8380416 | bytes 21037056 | tf_op jit(solution)/shard_map/reduce_sum | solution.py:82
  515.7 2.3 fusion.10
  (37 shorter events, 2.0 us)
Async XLA Ops:
  8.0 1.4 copy-start
  8.0 467.3 %reduce-scatter.2.cloned.1.call-start = ((), (), s32[]{:S(2)}) async-start(), calls=%async_computation.1 | async-start | bytes 557056 | tf_op jit(solution)/shard_map/reduce_scatter | solution.py:76
  40.3 8.0 %copy-start.2 = (f32[512,8192]{1,0:T(8,128)}, f32[512,8192]{1,0:T(8,128)S(1)}, u32[]{:S(2)}) copy-start(f32[512,8192]{1,0:T(8,128)S(1)} %multiply_exponential_fusion) | copy-start | bytes 50331652
  253.9 35.6 %copy-start.3 = (bf16[256,8192]{1,0:T(8,128)(2,1)S(1)}, bf16[256,8192]{1,0:T(8,128)(2,1)}, u32[]{:S(2)}) copy-start(bf16[256,8192]{1,0:T(8,128)(2,1)} %param.9) | copy-start | bytes 12582916
  289.5 38.4 %copy-start.7 = (u32[128]{0:T(128)S(1)}, u32[128]{0:T(128)}, u32[]{:S(2)}) copy-start(u32[128]{0:T(128)} %constant.44) | copy-start | bytes 1540
  289.5 39.6 %copy-start.6 = (bf16[32]{0:T(256)(128)(2,1)S(1)}, bf16[32]{0:T(256)(128)(2,1)}, u32[]{:S(2)}) copy-start(bf16[32]{0:T(256)(128)(2,1)} %param.11) | copy-start | bytes 196
  358.4 17.7 %copy-start.4 = (bf16[256,8192]{1,0:T(8,128)(2,1)S(1)}, bf16[256,8192]{1,0:T(8,128)(2,1)}, u32[]{:S(2)}) copy-start(bf16[256,8192]{1,0:T(8,128)(2,1)} %param.9) | copy-start | bytes 12582916
  372.9 3.2 copy-start.5
  379.3 130.5 %all-reduce.5.cloned.1.call-start = ((), (), s32[]{:S(2)}) async-start(), calls=%async_computation.2 | async-start | bytes 16777216 | tf_op jit(solution)/shard_map/psum | solution.py:81
  476.2 41.8 %copy-start.1 = (bf16[256,256]{1,0:T(8,128)(2,1)S(1)}, bf16[256,256]{1,0:T(8,128)(2,1)}, u32[]{:S(2)}) copy-start(bf16[256,256]{1,0:T(8,128)(2,1)} %param.7) | copy-start | bytes 393220
Sparse Core Ops, SparseCore 0:
  379.4 87.7 reduce-scatter.1
Sparse Core Ops, SparseCore 1:
  388.5 121.3 all-reduce.4
where the time goes:
time: 536 us; the launch traced here: 527 us
  blocking collectives  331 us (62%)
  matrix products  108 us (20%)
  waiting for transfers between devices  32.1 us (6%)
  other arithmetic  30.5 us (6%)
  between operations  18.9 us (4%)
  local copies, waits for them, and re-layouts  6.24 us (1%)
    psum x3, blocking collectives, on_device(): scale_rows = 1.0 / lax.psum(row_part, 'proto')  90.4 us
    psum x3, blocking collectives, on_device(): scale_cols = 1.0 / lax.psum(col_part, 'patch')  88 us
    psum x1, blocking collectives, on_device(): lax.psum((loss_partial, jnp.sum(row_weight.astype(jnp.float32))), ('patch...  85 us
    dot_general x3, matrix products, on_device(): row_part = jnp.dot(teacher_exp, scale_cols, precision=highest)  53 us
    psum x1, waiting for transfers between devices, on_device(): head_full = lax.psum(head_term(student_rows, grad_logits), 'patch')  32 us
    dot_general x3, matrix products, on_device(): col_part = jnp.dot(scale_rows, teacher_exp, precision=highest)  30.8 us
    unnamed x1, blocking collectives  29 us
    all_gather x1, blocking collectives, on_device(): lax.all_gather(own_teacher, 'proto', axis=0, tiled=True)  20.8 us
  transfers between devices with their start and end apart: 2, of which 1 were waited for; matrix products, arithmetic and copies ran while one was open for 2% of the time, Pallas kernels for 0%

commit v1 on v0

--- a/solution.py
+++ b/solution.py
@@ -7,6 +7,12 @@
 eps = 1e-06
 teacher_temp = 0.07
 student_temp = 0.1
+
+
+def gather_and_add(shard, axis):
+    terms = lax.all_gather(shard, axis, axis=0, tiled=False)
+    total = terms.sum(axis=0)
+    return total
 
 
 def unit_rows(values):
@@ -78,7 +84,7 @@
     )
     row_share = proto_unit.shape[0] // lax.axis_size("patch")
     row_offset = lax.axis_index("patch") * row_share
-    head_full = lax.psum(head_term(student_rows, grad_logits), "patch")
+    head_full = gather_and_add(head_term(student_rows, grad_logits), "patch")
     inner = jnp.sum(unit_proto * head_full, axis=0)
     whole_grad = col_inverse[None, :] * (head_full - unit_proto * inner[None, :])
     grad_proto = lax.dynamic_slice_in_dim(whole_grad, row_offset, row_share, 0)

time: 536 us -> 756 us (1.41)
  waiting for transfers between devices: 32.1 us -> 226 us
  other arithmetic: 30.5 us -> 54.9 us
    all_gather x0 -> x1, waiting for transfers between devices: none -> 226 us  [gather_and_add(): terms = lax.all_gather(shard, axis, axis=0, tiled=False)]
    psum x1 -> x0, waiting for transfers between devices: 32 us -> none  [on_device(): head_full = lax.psum(head_term(student_rows, grad_logits), 'patch')]
    reduce_sum x0 -> x1, other arithmetic: none -> 24.4 us  [gather_and_add(): total = terms.sum(axis=0)]
where the time goes in v1:
time: 756 us; the launch traced here: 746 us
  blocking collectives  331 us (44%)
  waiting for transfers between devices  226 us (30%)
  matrix products  108 us (14%)
  other arithmetic  54.9 us (7%)
  between operations  18.9 us (2%)
    all_gather x1, waiting for transfers between devices, gather_and_add(): terms = lax.all_gather(shard, axis, axis=0, tiled=False)  226 us
    psum x3, blocking collectives, on_device(): scale_cols = 1.0 / lax.psum(col_part, 'patch')  93.9 us
    psum x3, blocking collectives, on_device(): scale_rows = 1.0 / lax.psum(row_part, 'proto')  89.9 us
    psum x1, blocking collectives, on_device(): lax.psum((loss_partial, jnp.sum(row_weight.astype(jnp.float32))), ('patch...  80.2 us
    dot_general x3, matrix products, on_device(): row_part = jnp.dot(teacher_exp, scale_cols, precision=highest)  52.8 us
    dot_general x3, matrix products, on_device(): col_part = jnp.dot(scale_rows, teacher_exp, precision=highest)  30.8 us
    unnamed x1, blocking collectives  28.7 us
    reduce_sum x1, other arithmetic, gather_and_add(): total = terms.sum(axis=0)  24.4 us
  transfers between devices with their start and end apart: 2, of which 1 were waited for; matrix products, arithmetic and copies ran while one was open for 2% of the time, Pallas kernels for 0%

profile of v1, /device:TPU:1, one launch (start us, length us, event | category | flops | bytes accessed | tf_op | source)
XLA Modules:
  0.0 745.6 jit_solution(15844610642327376719)
XLA Ops:
  8.1 0.7 compare_select_fusion
  8.7 0.7 compare_and_fusion
  10.1 1.5 gather_fusion.1
  11.9 21.1 %all_gather.17 = bf16[512,256]{1,0:T(8,128)(2,1)S(1)} all-gather(bf16[32,256]{1,0:T(8,128)(2,1)S(1)} %get-tuple-element.15), channel_id=1, replica_groups=mesh['patch'=8,'proto'=16] {'proto'}, dimensions={0}, use_global_device_ids=true | all-gather | bytes 278528 | tf_op jit(solution)/shard_map/all_gather | solution.py:62
  33.0 3.1 fusion
  36.1 17.4 %all_gather.16 = bf16[512,256]{1,0:T(8,128)(2,1)S(1)} all-gather(bf16[32,256]{1,0:T(8,128)(2,1)S(1)} %get-tuple-element.14), channel_id=1, replica_groups=mesh['patch'=8,'proto'=16] {'proto'}, dimensions={0}, use_global_device_ids=true | all-gather | bytes 278528 | tf_op jit(solution)/shard_map/all_gather | solution.py:63
  53.5 4.5 multiply_exponential_fusion
  58.0 8.0 %exponential_reduce_fusion = (f32[512]{0:T(512)S(1)}, f32[512,8192]{1,0:T(8,128)}) fusion(bf16[512,256]{1,0:T(8,128)(2,1)S(1)} %all_gather.16, f32[8192]{0:T(1024)S(1)} %add_rsqrt_fusion, bf16[256,8192]{1,0:T(8,128)(2,1)S(1)} %copy-done.3), kind=kOutput, calls=%fused_computation.6 | convolution fusion | flops 2162163200 | bytes 21268480 | tf_op jit(solution)/shard_map/dot_general | solution.py:76
  65.9 7.9 %fusion.20 = f32[1,8192]{1,0:T(1,128)S(1)} fusion(f32[512,8192]{1,0:T(8,128)S(1)} %multiply_exponential_fusion), kind=kOutput, calls=%fused_computation.41 | convolution fusion | flops 50331648 | bytes 16809984 | tf_op jit(solution)/shard_map/dot_general | solution.py:72
  73.9 31.9 %psum.64 = f32[8192]{0:T(1024)S(1)} all-reduce(f32[8192]{0:T(1024)S(1)} %bitcast.34), channel_id=1, replica_groups=mesh['patch'=8,'proto'=16] {'patch'}, use_global_device_ids=true, to_apply=%region_5.7 | all-reduce | flops 8192 | bytes 65536 | tf_op jit(solution)/shard_map/psum | solution.py:73
  105.8 17.6 %fusion.23 = f32[1,512]{1,0:T(1,128)S(1)} fusion(f32[512,8192]{1,0:T(8,128)} %copy-done.2, f32[8192,1]{0,1:T(1,128)S(1)} %bitcast.30), kind=kOutput, calls=%fused_computation.50 | convolution fusion | flops 50331648 | bytes 16812032 | tf_op jit(solution)/shard_map/dot_general | solution.py:74
  123.4 31.0 %psum.65 = f32[512]{0:T(512)S(1)} all-reduce(f32[512]{0:T(512)S(1)} %bitcast.36), channel_id=1, replica_groups=mesh['patch'=8,'proto'=16] {'proto'}, use_global_device_ids=true, to_apply=%region_6.8 | all-reduce | flops 512 | bytes 4096 | tf_op jit(solution)/shard_map/psum | solution.py:75
  154.4 11.5 %fusion.24 = f32[1,8192]{1,0:T(1,128)S(1)} fusion(f32[512,1]{0,1:T(1,128)S(1)} %bitcast.38, f32[512,8192]{1,0:T(8,128)} %copy-done.2), kind=kOutput, calls=%fused_computation.51 | convolution fusion | flops 50331648 | bytes 16812032 | tf_op jit(solution)/shard_map/dot_general | solution.py:72
  165.9 30.9 %psum.66 = f32[8192]{0:T(1024)S(1)} all-reduce(f32[8192]{0:T(1024)S(1)} %bitcast.31), channel_id=1, replica_groups=mesh['patch'=8,'proto'=16] {'patch'}, use_global_device_ids=true, to_apply=%region_7.9 | all-reduce | flops 8192 | bytes 65536 | tf_op jit(solution)/shard_map/psum | solution.py:73
  196.8 17.6 %fusion.25 = f32[1,512]{1,0:T(1,128)S(1)} fusion(f32[512,8192]{1,0:T(8,128)} %copy-done.2, f32[8192,1]{0,1:T(1,128)S(1)} %bitcast.32), kind=kOutput, calls=%fused_computation.52 | convolution fusion | flops 50331648 | bytes 16812032 | tf_op jit(solution)/shard_map/dot_general | solution.py:74
  214.4 28.5 %psum.67 = f32[512]{0:T(512)S(1)} all-reduce(f32[512]{0:T(512)S(1)} %bitcast.37), channel_id=1, replica_groups=mesh['patch'=8,'proto'=16] {'proto'}, use_global_device_ids=true, to_apply=%region_8.10 | all-reduce | flops 512 | bytes 4096 | tf_op jit(solution)/shard_map/psum | solution.py:75
  242.9 11.5 %fusion.26 = f32[1,8192]{1,0:T(1,128)S(1)} fusion(f32[512,1]{0,1:T(1,128)S(1)} %bitcast.39, f32[512,8192]{1,0:T(8,128)} %copy-done.2), kind=kOutput, calls=%fused_computation.53 | convolution fusion | flops 50331648 | bytes 16812032 | tf_op jit(solution)/shard_map/dot_general | solution.py:72
  254.4 31.1 %psum.68 = f32[8192]{0:T(1024)S(1)} all-reduce(f32[8192]{0:T(1024)S(1)} %bitcast.33), channel_id=1, replica_groups=mesh['patch'=8,'proto'=16] {'patch'}, use_global_device_ids=true, to_apply=%region_9.11 | all-reduce | flops 8192 | bytes 65536 | tf_op jit(solution)/shard_map/psum | solution.py:73
  285.5 17.6 %fusion.27 = f32[1,512]{1,0:T(1,128)S(1)} fusion(f32[512,8192]{1,0:T(8,128)} %copy-done.2, f32[8192,1]{0,1:T(1,128)S(1)} %bitcast.29), kind=kOutput, calls=%fused_computation.54 | convolution fusion | flops 50331648 | bytes 16812032 | tf_op jit(solution)/shard_map/dot_general | solution.py:74
  303.1 30.4 %all-reduce.2 = (f32[512]{0:T(512)S(1)}, f32[512]{0:T(512)S(1)}) all-reduce(f32[512]{0:T(512)S(1)} %bitcast.35, f32[512]{0:T(512)S(1)} %get-tuple-element.16), channel_id=1, replica_groups=mesh['patch'=8,'proto'=16] {'proto'}, use_global_device_ids=true, to_apply=%region_10.12 | all-reduce | flops 1024 | bytes 8192 | tf_op jit(solution)/shard_map/psum | solution.py:75
  335.0 28.7 %all-reduce = bf16[512]{0:T(512)(128)(2,1)S(1)} all-reduce(bf16[512]{0:T(512)(128)(2,1)S(1)} %dynamic-update-slice), channel_id=1, replica_groups=mesh['patch'=8,'proto'=16] {'proto'}, use_global_device_ids=true, to_apply=%add | all-reduce | flops 512 | bytes 2048
  363.7 14.4 %multiply_reduce_fusion = (f32[]{:T(128)}, bf16[512,8192]{1,0:T(8,128)(2,1)S(1)}) fusion(f32[512,8192]{1,0:T(8,128)} %copy-done.2, f32[512,8192]{1,0:T(8,128)} %get-tuple-element.17, f32[512]{0:T(512)S(1)} %log.3, f32[8192]{0:T(1024)S(1)} %broadcast_divide_fusion, f32[512]{0:T(512)S(1)} %broadcast_divide_fusion.5, f32[512]{0:T(512)S(1)} %convert_element_type.28, ...), kind=kLoop, calls=%fused_computation.2 | loop fusion | flops 46137344 | bytes 41984004 | tf_op jit(solution)/shard_map/reduce_sum | solution.py:29
  378.2 3.2 copy-done.5
  381.4 3.2 fusion.7
  384.8 8.9 %convolution_multiply_fusion = f32[256,8192]{1,0:T(8,128)} fusion(bf16[512,256]{1,0:T(8,128)(2,1)S(1)} %all_gather.16, bf16[512,8192]{1,0:T(8,128)(2,1)} %copy-done.5), kind=kOutput, calls=%fused_computation.7 | convolution fusion | flops 2149580800 | bytes 17039360 | tf_op jit(solution)/shard_map/dot_general | solution.py:44
  394.4 80.2 %all-reduce.1 = (f32[]{:T(128)}, f32[]{:T(128)}) all-reduce(f32[]{:T(128)} %get-tuple-element.10, f32[]{:T(128)} %convert_reduce_fusion), channel_id=1, replica_groups=mesh['patch'=8,'proto'=16] {'patch','proto'}, use_global_device_ids=true, to_apply=%region_16.18 | all-reduce | flops 2 | bytes 16 | tf_op jit(solution)/shard_map/psum | solution.py:91
  475.9 1.0 fusion.14
  476.9 1.5 fusion.16
  478.4 225.8 %all-gather.3.cloned.1.call-done = f32[2048,8192]{1,0:T(8,128)} async-done(((f32[256,8192]{1,0:T(8,128)}), f32[2048,8192]{1,0:T(8,128)}) %all-gather.3.cloned.1.call-update) | async-done | bytes 67108880 | tf_op jit(solution)/shard_map/all_gather | solution.py:13
  704.2 24.4 %reduce_sum.86 = f32[256,8192]{1,0:T(8,128)} reduce(f32[8,256,8192]{2,1,0:T(8,128)} %bitcast.12, f32[]{:T(128)} %constant.18.clone.1), dimensions={0}, to_apply=%region_13.15 | reduce | flops 14680064 | bytes 75497472 | tf_op jit(solution)/shard_map/reduce_sum | solution.py:14
  728.6 6.0 multiply_reduce_fusion.1
  734.5 2.3 fusion.10
  (38 shorter events, 2.8 us)
Async XLA Ops:
  8.0 1.4 copy-start
  8.0 467.9 %reduce-scatter.2.cloned.1.call-start = ((), (), s32[]{:S(2)}) async-start(), calls=%async_computation.1 | async-start | bytes 557056 | tf_op jit(solution)/shard_map/reduce_scatter | solution.py:82
  11.6 46.4 %copy-start.3 = (bf16[256,8192]{1,0:T(8,128)(2,1)S(1)}, bf16[256,8192]{1,0:T(8,128)(2,1)}, u32[]{:S(2)}) copy-start(bf16[256,8192]{1,0:T(8,128)(2,1)} %param.9) | copy-start | bytes 12582916
  58.0 15.9 %copy-start.2 = (f32[512,8192]{1,0:T(8,128)}, f32[512,8192]{1,0:T(8,128)S(1)}, u32[]{:S(2)}) copy-start(f32[512,8192]{1,0:T(8,128)S(1)} %multiply_exponential_fusion) | copy-start | bytes 50331652
  254.4 79.1 %copy-start.7 = (u32[128]{0:T(128)S(1)}, u32[128]{0:T(128)}, u32[]{:S(2)}) copy-start(u32[128]{0:T(128)} %constant.44) | copy-start | bytes 1540
  254.4 80.4 %copy-start.6 = (bf16[32]{0:T(256)(128)(2,1)S(1)}, bf16[32]{0:T(256)(128)(2,1)}, u32[]{:S(2)}) copy-start(bf16[32]{0:T(256)(128)(2,1)} %param.11) | copy-start | bytes 196
  363.7 17.7 %copy-start.4 = (bf16[256,8192]{1,0:T(8,128)(2,1)S(1)}, bf16[256,8192]{1,0:T(8,128)(2,1)}, u32[]{:S(2)}) copy-start(bf16[256,8192]{1,0:T(8,128)(2,1)} %param.9) | copy-start | bytes 12582916
  378.1 3.2 copy-start.5
  384.6 319.6 %all-gather.3.cloned.1.call-start = ((), (), s32[]{:S(2)}) async-start(), calls=%async_computation.2 | async-start | bytes 75497472 | tf_op jit(solution)/shard_map/all_gather | solution.py:13
  704.2 32.7 %copy-start.1 = (bf16[256,256]{1,0:T(8,128)(2,1)S(1)}, bf16[256,256]{1,0:T(8,128)(2,1)}, u32[]{:S(2)}) copy-start(bf16[256,256]{1,0:T(8,128)(2,1)} %param.7) | copy-start | bytes 393220
Sparse Core Ops, SparseCore 0:
  384.7 83.1 reduce-scatter.1
Sparse Core Ops, SparseCore 1:
  393.9 310.3 all-gather.2
